TPU v7x, 256 devices: a whole 4x4x8 slice. The times are simulated.
256 devices in a mesh: seq: 64 (over x, z, core), head: 4 (over y).
Axes of the slice: x: 4, y: 4, z: 8, core: 2. Of those that a mesh axis runs over, the one named last changes fastest.
Arguments:
- tokens: bfloat16 [65536, 2048], P('seq', 'head'), may hold values from -6 to 6
- w_qkv: bfloat16 [2048, 6144], P(None, 'head'), may hold values from -1 to 1
- item_at: int32 [4, 2048], P('head'), may hold values from 0 to 2047, as said below
- rand_cols: int32 [16, 512, 4], P('head'), may hold values from 0 to 511, as said below
- rand_used: int32 [16, 512], P('head'), may hold values from 0 to 4, as said below
Outputs:
- attended: bfloat16 [4, 2048, 128, 128], P('head', 'seq')
Inputs may be any that keep to these rules, and one draw needn't show every extreme that they name: In head group g, item e * 512 + r stands for head g * 4 + e at block row r, and every item appears exactly once in item_at[g]. Positions j * 32 to (j + 1) * 32 - 1 hold the items placed at device j of seq. Of the items whose block rows lie on one device of seq, at most 1 of one group are placed at any one device, and exactly 1 at some. `rand_cols`: take all 128 candidates (used or not) of the items placed at one device in one head group, or of the items of one group whose block rows lie on one device: at most 2 of them lie in the block rows of any one device of seq, and exactly 2 in some. A candidate may equal a window block or block 0. `rand_used`: in each head group the counts of the 32 items placed at one device sum to exactly 64; the sums over the items whose block rows lie on one device vary.
All inputs are finite; a program needn't handle non-finite values.
Results may differ from a plain program's by a relative error of at most 0.019.
Values may be sent and summed in bfloat16 or wider, within the bound.
No kernel may reach another device: no remote copies, remote signals or barrier semaphores. Data moves between devices by JAX's collectives and lax.ppermute only.
A program may use at most 128 MiB of HBM per device.

v0:
```python
import math
import jax
import jax.numpy as jnp
from jax import lax
from jax.sharding import PartitionSpec as P

neg_large = -1e30


def extended(block, sides, width):
    for axis, dim in sides:
        count = lax.axis_size(axis)
        forward = [(i, i + 1) for i in range(count - 1)]
        backward = [(target, source) for source, target in forward]
        low = lax.ppermute(
            lax.slice_in_dim(block, block.shape[dim] - width, None, axis=dim), axis, forward
        )
        high = lax.ppermute(lax.slice_in_dim(block, 0, width, axis=dim), axis, backward)
        block = jnp.concatenate([low, block, high], axis=dim)
    return block


def broadcast(block, axis, owner):
    block = jnp.where(lax.axis_index(axis) == owner, block, jnp.zeros_like(block))
    return lax.psum(block, axis)


def packed_attend(
    queries, near_keys, near_values, near_usable, rand_keys, rand_values, slot_item, factor
):
    item_count = queries.shape[0]
    near_scores = (
        jnp.einsum("ibe,ijke->ibjk", queries, near_keys, preferred_element_type=jnp.float32)
        * factor
    )
    near_scores = jnp.where(near_usable[:, None, :, None], near_scores, neg_large)
    rand_scores = (
        jnp.einsum(
            "kbe,kce->kbc", queries[slot_item], rand_keys, preferred_element_type=jnp.float32
        )
        * factor
    )
    member = slot_item[None, :] == jnp.arange(item_count, dtype=jnp.int32)[:, None]
    slot_max = jnp.max(rand_scores, axis=2)
    rand_max = jnp.max(jnp.where(member[:, :, None], slot_max[None], neg_large), axis=1)
    row_max = jnp.maximum(jnp.max(near_scores, axis=(2, 3)), rand_max)
    near_expo = jnp.exp(near_scores - row_max[:, :, None, None])
    rand_expo = jnp.exp(rand_scores - row_max[slot_item][:, :, None])
    slot_total = jnp.sum(rand_expo, axis=2)
    row_sum = jnp.sum(near_expo, axis=(2, 3)) + jnp.sum(
        jnp.where(member[:, :, None], slot_total[None], 0.0), axis=1
    )
    summed = jnp.einsum(
        "ibjk,ijke->ibe",
        near_expo.astype(jnp.bfloat16),
        near_values,
        preferred_element_type=jnp.float32,
    )
    slot_out = jnp.einsum(
        "kbc,kce->kbe",
        rand_expo.astype(jnp.bfloat16),
        rand_values,
        preferred_element_type=jnp.float32,
    )
    summed = summed + jnp.einsum(
        "ik,kbe->ibe", member.astype(jnp.float32), slot_out, precision=lax.Precision.HIGHEST
    )
    return (summed, row_max, row_sum)


def rank_among(homes):
    count = homes.shape[-1]
    earlier = jnp.tril(jnp.ones((count, count), bool), -1)
    same_home = homes[..., :, None] == homes[..., None, :]
    return jnp.sum(same_home & earlier, axis=-1)


def pack_live(counts, rand_count, live_total):
    slot_total = counts.shape[0] * rand_count
    slot_ids = jnp.arange(slot_total, dtype=jnp.int32)
    live = slot_ids % rand_count < jnp.repeat(counts, rand_count)
    live_rank = jnp.cumsum(live.astype(jnp.int32)) - 1
    picks = live[:, None] & (live_rank[:, None] == jnp.arange(live_total, dtype=jnp.int32)[None, :])
    return jnp.sum(jnp.where(picks, slot_ids[:, None], 0), axis=0)


def local(tokens, w_qkv, item_at, rand_cols, rand_used):
    seq_count = lax.axis_size("seq")
    my_seq = lax.axis_index("seq")
    heads_dev, nblocks, rand_count = rand_cols.shape
    tokens_dev = tokens.shape[0]
    head_dim = w_qkv.shape[1] // (3 * heads_dev)
    block_len = tokens_dev * seq_count // nblocks
    rows_dev = tokens_dev // block_len
    items_dev = heads_dev * rows_dev
    slot_count = items_dev * rand_count
    live_total = slot_count // 2
    cap_items = max(1, items_dev // seq_count)
    cap_tiles = max(1, slot_count // seq_count)
    factor = 1.0 / math.sqrt(head_dim)
    projected = jnp.dot(
        lax.all_gather(tokens, "head", axis=1, tiled=True),
        w_qkv,
        preferred_element_type=jnp.float32,
    )
    projected = projected.astype(jnp.bfloat16).reshape(rows_dev, block_len, 3, heads_dev, head_dim)
    query_tiles = projected[:, :, 0].transpose(2, 0, 1, 3).reshape(items_dev, block_len, head_dim)
    pair_rows = projected[:, :, 1:].reshape(tokens_dev, 2, heads_dev, head_dim)
    widened = extended(pair_rows, (("seq", 0),), block_len)
    pair_tiles = widened.reshape(rows_dev + 2, block_len, 2, heads_dev, head_dim).transpose(
        3, 0, 2, 1, 4
    )
    own_tiles = pair_tiles[:, 1 : rows_dev + 1].reshape(items_dev, 2, block_len, head_dim)
    first_tiles = broadcast(pair_tiles[:, 1], "seq", 0)
    window_tiles = jnp.stack(
        [
            pair_tiles[:, 0:rows_dev],
            pair_tiles[:, 1 : rows_dev + 1],
            pair_tiles[:, 2 : rows_dev + 2],
        ],
        axis=2,
    )
    window_tiles = window_tiles.reshape(items_dev, 3, 2, block_len, head_dim)
    placed = item_at[0].reshape(seq_count, items_dev)
    placed_head = placed // nblocks
    placed_row = placed % nblocks
    placed_home = placed_row // rows_dev
    local_index = placed_head * rows_dev + placed_row % rows_dev
    is_mine = placed_home == my_seq
    rank_mine = jnp.cumsum(is_mine.astype(jnp.int32), axis=1) - 1
    slot_ids = jnp.arange(cap_items, dtype=jnp.int32)
    slot_hit = is_mine[:, :, None] & (rank_mine[:, :, None] == slot_ids)
    send_index = jnp.sum(jnp.where(slot_hit, local_index[:, :, None], 0), axis=1).reshape(-1)
    my_items = lax.dynamic_index_in_dim(placed, my_seq, 0, keepdims=False)
    item_head = my_items // nblocks
    item_row = my_items % nblocks
    item_home = item_row // rows_dev
    recv_slot = item_home * cap_items + rank_among(item_home)
    my_random = rand_cols[item_head, item_row].reshape(-1)
    tile_home = my_random // rows_dev
    tile_rank = rank_among(tile_home)
    tile_slot = tile_home * cap_tiles + tile_rank
    tile_ids = jnp.arange(cap_tiles, dtype=jnp.int32)
    peer_ids = jnp.arange(seq_count, dtype=jnp.int32)
    slot_head = jnp.repeat(item_head, rand_count)
    tile_local = slot_head * rows_dev + my_random % rows_dev
    wanted = (tile_home[None, :, None] == peer_ids[:, None, None]) & (
        tile_rank[None, :, None] == tile_ids[None, None, :]
    )
    requests = jnp.sum(jnp.where(wanted, tile_local[None, :, None], 0), axis=1)
    asked = lax.all_to_all(requests, "seq", split_axis=0, concat_axis=0, tiled=True)
    picked = own_tiles[asked.reshape(-1)].reshape(asked.shape + own_tiles.shape[1:])
    fetched = lax.all_to_all(picked, "seq", split_axis=0, concat_axis=0, tiled=True)
    gathered = fetched.reshape(seq_count * cap_tiles, 2, block_len, head_dim)[tile_slot]
    random_tiles = gathered.reshape(items_dev, rand_count, 2, block_len, head_dim)
    item_counts = rand_used[item_head, item_row]
    live_slots = pack_live(item_counts, rand_count, live_total)
    packed_tiles = random_tiles.reshape(slot_count, 2, block_len, head_dim)[live_slots]
    slot_item = live_slots // rand_count
    global_tiles = first_tiles[item_head][:, None]
    sent_query = query_tiles[send_index].reshape(seq_count, cap_items, block_len, head_dim)
    sent_window = window_tiles[send_index].reshape(seq_count, cap_items, 3, 2, block_len, head_dim)
    got_query, got_window = (
        lax.all_to_all(sent_query, "seq", split_axis=0, concat_axis=0, tiled=True),
        lax.all_to_all(sent_window, "seq", split_axis=0, concat_axis=0, tiled=True),
    )
    queries = got_query.reshape(seq_count * cap_items, block_len, head_dim)[recv_slot]
    windows = got_window.reshape(seq_count * cap_items, 3, 2, block_len, head_dim)[recv_slot]
    near_tiles = jnp.concatenate([windows, global_tiles], axis=1)
    near_usable = jnp.concatenate(
        [
            (item_row >= 1)[:, None],
            jnp.ones((items_dev, 1), bool),
            (item_row + 1 < nblocks)[:, None],
            jnp.ones((items_dev, 1), bool),
        ],
        axis=1,
    )
    summed, row_max, row_sum = packed_attend(
        queries,
        near_tiles[:, :, 0],
        near_tiles[:, :, 1],
        near_usable,
        packed_tiles[:, 0],
        packed_tiles[:, 1],
        slot_item,
        factor,
    )
    result = (summed / row_sum[:, :, None]).astype(jnp.bfloat16)
    return result.reshape(1, items_dev, block_len, head_dim)


def solution(mesh):
    return jax.shard_map(
        local,
        mesh=mesh,
        in_specs=(
            P("seq", "head"),
            P(None, "head"),
            P("head", None),
            P("head", None, None),
            P("head", None),
        ),
        out_specs=P("head", "seq", None, None),
        check_vma=False,
    )
```

profile of v0, /device:TPU:1, one launch (start us, length us, event | category | flops | bytes accessed | tf_op | source)
XLA Modules:
  0.0 679.1 jit_solution(8968216010016144075)
XLA Ops:
  6.5 0.7 all-gather.2.cloned.1.call-update
  7.3 0.5 broadcast.1180
  7.8 1.3 reduce.15
  9.2 1.1 copy.117
  10.4 0.2 convert_reduce_fusion.1
  10.6 0.6 fusion.78
  11.2 0.7 gather_fusion.7
  12.2 0.2 convert_reduce_fusion
  12.5 0.7 copy.118
  13.3 13.0 %all-to-all-start.2 = ((s32[64,1,2]{2,1,0:T(1,128)}), s32[64,1,2]{2,1,0:T(1,128)S(1)}, u32[]{:S(2)}, u32[]{:S(2)}) async-start(s32[64,1,2]{2,1,0:T(1,128)} %copy.118), calls=%async_computation.2 | async-start | bytes 65536 | tf_op jit(solution)/shard_map/all_to_all | solution.py:151
  26.3 0.2 reduce_window_sum.18
  26.5 0.8 reshape_squeeze.6
  27.5 36.4 %all-gather.2.cloned.1.call-done = bf16[1024,2048]{1,0:T(8,128)(2,1)} async-done(((bf16[1024,512]{1,0:T(8,128)(2,1)}), bf16[1024,2048]{1,0:T(8,128)(2,1)}) %all-gather.2.cloned.1.call-update) | async-done | bytes 4194320 | tf_op jit(solution)/shard_map/all_gather | solution.py:102
  63.8 11.2 %convolution_convert_fusion = bf16[1024,1536]{1,0:T(8,128)(2,1)} fusion(bf16[1024,2048]{1,0:T(8,128)(2,1)} %all-gather.2.cloned.1.call-done, bf16[2048,1536]{1,0:T(8,128)(2,1)} %param.6), kind=kOutput, calls=%fused_computation.35 | convolution fusion | flops 6444023808 | bytes 13631488 | tf_op jit(solution)/shard_map/dot_general | solution.py:101
  75.0 5.0 reshape.931
  80.0 0.4 slice.83
  80.4 1.2 copy.137
  81.6 3.3 gather_fusion
  85.0 10.9 %all-to-all-start = ((bf16[64,1,128,128]{3,2,1,0:T(8,128)(2,1)}), bf16[64,1,128,128]{3,2,1,0:T(8,128)(2,1)}, u32[]{:S(2)}, u32[]{:S(2)}) async-start(bf16[64,1,128,128]{3,2,1,0:T(8,128)(2,1)} %bitcast.166), calls=%async_computation | async-start | bytes 4194304 | tf_op jit(solution)/shard_map/all_to_all | solution.py:164
  95.9 0.2 fusion.85
  96.0 0.7 copy.160
  96.8 3.5 collective-permute-start
  100.3 0.7 copy.159
  101.1 2.1 collective-permute-start.1
  103.2 0.7 reduce.16
  104.1 0.7 slice.85
  104.8 0.5 copy.106
  105.3 38.3 %collective-permute-done = bf16[128,2,4,128]{3,0,2,1:T(8,128)(2,1)S(1)} collective-permute-done((bf16[128,2,4,128]{3,0,2,1:T(8,128)(2,1)}, bf16[128,2,4,128]{3,0,2,1:T(8,128)(2,1)S(1)}, u32[]{:S(2)}, u32[]{:S(2)}) %collective-permute-start) | collective-permute-done | bytes 262176 | tf_op jit(solution)/shard_map/ppermute | solution.py:15
  143.6 2.4 collective-permute-done.1
  146.0 1.1 pad_maximum_fusion.2
  147.1 0.3 copy.157
  147.5 3.7 fusion.86
  151.4 6.7 gather_fusion.8
  158.0 9.3 %all-to-all-start.3 = ((bf16[64,2,2,128,128]{4,3,2,1,0:T(8,128)(2,1)}), bf16[64,2,2,128,128]{4,3,2,1,0:T(8,128)(2,1)}, u32[]{:S(2)}, u32[]{:S(2)}) async-start(bf16[64,2,2,128,128]{4,3,2,1,0:T(8,128)(2,1)} %bitcast.161), calls=%async_computation.3 | async-start | bytes 16777216 | tf_op jit(solution)/shard_map/all_to_all | solution.py:153
  167.4 1.9 copy.109
  169.2 0.3 copy-done.5
  169.6 0.2 copy.111
  169.8 3.3 pad_maximum_fusion
  173.1 10.0 %gather_fusion.2 = bf16[64,3,2,128,128]{4,3,2,1,0:T(8,128)(2,1)} fusion(bf16[32,3,2,128,128]{4,3,2,0,1:T(8,128)(2,1)} %pad_maximum_fusion, s32[1024]{0:T(1024)S(1)} %pad_clamp_fusion.6), kind=kCustom, calls=%fused_computation.2 | custom fusion | bytes 25166080 | tf_op jit(solution)/shard_map/gather | solution.py:162
  183.1 170.1 %all-to-all-done.3 = bf16[64,2,2,128,128]{4,3,2,1,0:T(8,128)(2,1)} async-done(((bf16[64,2,2,128,128]{4,3,2,1,0:T(8,128)(2,1)}), bf16[64,2,2,128,128]{4,3,2,1,0:T(8,128)(2,1)}, u32[]{:S(2)}, u32[]{:S(2)}) %all-to-all-start.3) | async-done | bytes 8388640 | tf_op jit(solution)/shard_map/all_to_all | solution.py:153
  353.1 6.2 all-to-all-start.1
  359.3 0.3 all-reduce.2.cloned.1.call-start
  359.7 0.8 gather_fusion.5
  361.5 1.7 fusion.37
  363.3 221.0 %all-reduce.2.cloned.1.call-done = bf16[4,2,128,128]{3,2,1,0:T(8,128)(2,1)} async-done(((bf16[4,2,128,128]{3,2,1,0:T(8,128)(2,1)}), bf16[4,2,128,128]{3,2,1,0:T(8,128)(2,1)}) %all-reduce.2.cloned.1.call-update) | async-done | bytes 262160 | tf_op jit(solution)/shard_map/psum | solution.py:25
  584.3 1.9 gather_fusion.4
  586.2 1.5 copy.158
  587.7 2.3 gather_fusion.1
  590.1 1.0 gather_fusion.6
  591.0 10.0 %gather_fusion.9 = bf16[128,2,128,128]{3,2,1,0:T(8,128)(2,1)} fusion(bf16[128,2,128,128]{3,2,1,0:T(8,128)(2,1)} %bitcast.37, s32[1024]{0:T(1024)S(1)} %pad_clamp_fusion.1), kind=kCustom, calls=%fused_computation.9 | custom fusion | bytes 16777728 | tf_op jit(solution)/shard_map/gather | solution.py:154
  601.0 6.4 gather_fusion.10
  607.4 5.2 multiply_reduce_fusion
  612.7 0.4 select_reduce_fusion.1
  613.1 25.2 %all-to-all-done.1 = bf16[64,1,3,2,128,128]{5,4,3,2,1,0:T(8,128)(2,1)} async-done(((bf16[64,1,3,2,128,128]{5,4,3,2,1,0:T(8,128)(2,1)}), bf16[64,1,3,2,128,128]{5,4,3,2,1,0:T(8,128)(2,1)}, u32[]{:S(2)}, u32[]{:S(2)}) %all-to-all-start.1) | async-done | bytes 12582944 | tf_op jit(solution)/shard_map/all_to_all | solution.py:165
  638.3 8.7 %gather_fusion.3 = bf16[32,3,2,128,128]{4,3,2,1,0:T(8,128)(2,1)} fusion(bf16[64,3,2,128,128]{4,3,2,1,0:T(8,128)(2,1)} %bitcast.26, s32[1024]{0:T(1024)S(1)} %pad_clamp_fusion.5), kind=kCustom, calls=%fused_computation.3 | custom fusion | bytes 12583040 | tf_op jit(solution)/shard_map/gather | solution.py:168
  647.0 5.5 fusion
  652.5 0.6 gather_fusion.11
  653.1 3.3 fusion.18
  656.6 2.7 fusion.20
  659.3 0.4 select_reduce_fusion
  659.7 0.9 copy-done.4
  660.6 2.1 fusion.1
  662.7 4.1 fusion.12
  666.8 5.5 fusion.31
  (68 shorter events, 2.5 us)
Async XLA Ops:
  6.5 353.1 %copy-start = (s32[4,512]{1,0:T(4,128)S(1)}, s32[4,512]{1,0:T(4,128)}, u32[]{:S(2)}) copy-start(s32[4,512]{1,0:T(4,128)} %param.9) | copy-start | bytes 24580
  6.5 57.3 %all-gather.2.cloned.1.call-start = ((), (), s32[]{:S(2)}) async-start(), calls=%async_computation.4 | async-start | bytes 5242880 | tf_op jit(solution)/shard_map/all_gather | solution.py:102
  13.3 71.7 %all-to-all-start.2 = ((s32[64,1,2]{2,1,0:T(1,128)}), s32[64,1,2]{2,1,0:T(1,128)S(1)}, u32[]{:S(2)}, u32[]{:S(2)}) async-start(s32[64,1,2]{2,1,0:T(1,128)} %copy.118), calls=%async_computation.2 | async-start | bytes 65536 | tf_op jit(solution)/shard_map/all_to_all | solution.py:151
  85.0 73.1 %all-to-all-start = ((bf16[64,1,128,128]{3,2,1,0:T(8,128)(2,1)}), bf16[64,1,128,128]{3,2,1,0:T(8,128)(2,1)}, u32[]{:S(2)}, u32[]{:S(2)}) async-start(bf16[64,1,128,128]{3,2,1,0:T(8,128)(2,1)} %bitcast.166), calls=%async_computation | async-start | bytes 4194304 | tf_op jit(solution)/shard_map/all_to_all | solution.py:164
  96.8 46.8 %collective-permute-start = (bf16[128,2,4,128]{3,0,2,1:T(8,128)(2,1)}, bf16[128,2,4,128]{3,0,2,1:T(8,128)(2,1)S(1)}, u32[]{:S(2)}, u32[]{:S(2)}) collective-permute-start(bf16[128,2,4,128]{3,0,2,1:T(8,128)(2,1)} %bitcast.157), channel_id=1, source_target_pairs={{0,4},{4,8},{8,12},{12,16},{16,20},{20,24},{24,28},{28,32},{32,36}... | collective-permute-start | bytes 786440 | tf_op jit(solution)/shard_map/ppermute | solution.py:15
  101.1 44.9 %collective-permute-start.1 = (bf16[128,2,4,128]{3,0,2,1:T(8,128)(2,1)}, bf16[128,2,4,128]{3,0,2,1:T(8,128)(2,1)}, u32[]{:S(2)}, u32[]{:S(2)}) collective-permute-start(bf16[128,2,4,128]{3,0,2,1:T(8,128)(2,1)} %bitcast.156), channel_id=1, source_target_pairs={{4,0},{8,4},{12,8},{16,12},{20,16},{24,20},{28,24},{32,28},{36,32}... | collective-permute-start | bytes 786440 | tf_op jit(solution)/shard_map/ppermute | solution.py:18
  147.5 3.8 copy-start.3
  158.0 195.1 %all-to-all-start.3 = ((bf16[64,2,2,128,128]{4,3,2,1,0:T(8,128)(2,1)}), bf16[64,2,2,128,128]{4,3,2,1,0:T(8,128)(2,1)}, u32[]{:S(2)}, u32[]{:S(2)}) async-start(bf16[64,2,2,128,128]{4,3,2,1,0:T(8,128)(2,1)} %bitcast.161), calls=%async_computation.3 | async-start | bytes 16777216 | tf_op jit(solution)/shard_map/all_to_all | solution.py:153
  167.3 2.2 copy-start.5
  353.1 7.9 %copy-start.7 = (s32[32]{0:T(128)S(1)}, s32[32]{0:T(128)}, u32[]{:S(2)}) copy-start(s32[32]{0:T(128)} %get-tuple-element.21) | copy-start | bytes 388
  353.1 285.1 %all-to-all-start.1 = ((bf16[64,1,3,2,128,128]{5,4,3,2,1,0:T(8,128)(2,1)}), bf16[64,1,3,2,128,128]{5,4,3,2,1,0:T(8,128)(2,1)}, u32[]{:S(2)}, u32[]{:S(2)}) async-start(bf16[64,1,3,2,128,128]{5,4,3,2,1,0:T(8,128)(2,1)} %bitcast.160), calls=%async_computation.1 | async-start | bytes 25165824 | tf_op jit(solution)/shard_map/all_to_all | solution.py:165
  359.3 225.0 %all-reduce.2.cloned.1.call-start = ((), (), s32[]{:S(2)}) async-start(), calls=%async_computation.5 | async-start | bytes 524288 | tf_op jit(solution)/shard_map/psum | solution.py:25
  638.3 8.7 %copy-start.6 = (bf16[32,2,128,128]{3,2,0,1:T(8,128)(2,1)S(1)}, bf16[32,2,128,128]{3,2,0,1:T(8,128)(2,1)}, u32[]{:S(2)}) copy-start(bf16[32,2,128,128]{3,2,0,1:T(8,128)(2,1)} %copy.158) | copy-start | bytes 6291460
  653.1 3.4 copy-start.2
  656.6 4.0 copy-start.4
  656.6 10.2 %slice-start = ((s8[6291456]{0:T(1024)(128)(4,1)}), s8[4194304]{0:T(1024)(128)(4,1)S(1)}, s32[]{:S(2)}) async-start(s8[6291456]{0:T(1024)(128)(4,1)} %bitcast.170), calls=%async_computation.6 | async-start | bytes 8388608
  660.6 6.2 slice-start.1
  666.8 5.5 copy-start.1
Sparse Core Ops, SparseCore 0:
  9.2 54.5 all-gather.1
  363.6 220.6 all-reduce.1
where the time goes:
time: 680 us; the launch traced here: 679 us
  waiting for transfers between devices  494 us (73%)
  local copies, waits for them, and re-layouts  75.2 us (11%)
  starting transfers between devices  45.3 us (7%)
  matrix products  34.2 us (5%)
  other arithmetic  16.5 us (2%)
  between operations  13.8 us (2%)
    psum x1, waiting for transfers between devices, broadcast(): return lax.psum(block, axis)  221 us
    all_to_all x1, waiting for transfers between devices, local(): lax.all_to_all(picked, 'seq', split_axis=0, concat_axis=0, tiled=True)  170 us
    ppermute x1, waiting for transfers between devices, extended(): lax.ppermute(lax.slice_in_dim(block, block.shape[dim] - width, None, axis...  38.3 us
    all_gather x1, waiting for transfers between devices, local(): lax.all_gather(tokens, 'head', axis=1, tiled=True)  36.4 us
    all_to_all x1, waiting for transfers between devices, local(): lax.all_to_all(sent_window, 'seq', split_axis=0, concat_axis=0, tiled=True)  25.2 us
  transfers between devices with their start and end apart: 8, of which 6 were waited for; matrix products, arithmetic and copies ran while one was open for 14% of the time, Pallas kernels for 0%

commit v1 on v0

--- a/solution.py
+++ b/solution.py
@@ -22,7 +22,7 @@
 
 def broadcast(block, axis, owner):
     block = jnp.where(lax.axis_index(axis) == owner, block, jnp.zeros_like(block))
-    return lax.psum(block, axis)
+    return jnp.sum(lax.all_gather(block, axis), axis=0)
 
 
 def packed_attend(

time: 680 us -> 734 us (1.079)
  waiting for transfers between devices: 494 us -> 544 us
    all_to_all x1, waiting for transfers between devices: 25.2 us -> 248 us  [local(): lax.all_to_all(sent_window, 'seq', split_axis=0, concat_axis=0, tiled=True)]
    psum x1 -> x0, waiting for transfers between devices: 221 us -> none  [broadcast(): return lax.psum(block, axis)]
    all_to_all x1, waiting for transfers between devices: 170 us -> 217 us  [local(): lax.all_to_all(picked, 'seq', split_axis=0, concat_axis=0, tiled=True)]
  transfers between devices with their start and end apart: 8 -> 8, of which waited for: 6 -> 5; matrix products, arithmetic and copies ran while one was open for 14% -> 13% of each run, Pallas kernels for 0% -> 0%
where the time goes in v1:
time: 734 us; the launch traced here: 733 us
  waiting for transfers between devices  544 us (74%)
  local copies, waits for them, and re-layouts  72.6 us (10%)
  starting transfers between devices  44.9 us (6%)
  matrix products  34.7 us (5%)
  other arithmetic  22.6 us (3%)
  between operations  13.9 us (2%)
    all_to_all x1, waiting for transfers between devices, local(): lax.all_to_all(sent_window, 'seq', split_axis=0, concat_axis=0, tiled=True)  248 us
    all_to_all x1, waiting for transfers between devices, local(): lax.all_to_all(picked, 'seq', split_axis=0, concat_axis=0, tiled=True)  217 us
    ppermute x1, waiting for transfers between devices, extended(): lax.ppermute(lax.slice_in_dim(block, block.shape[dim] - width, None, axis...  38.3 us
    all_gather x1, waiting for transfers between devices, local(): lax.all_gather(tokens, 'head', axis=1, tiled=True)  37 us
  transfers between devices with their start and end apart: 8, of which 5 were waited for; matrix products, arithmetic and copies ran while one was open for 13% of the time, Pallas kernels for 0%

profile of v1, /device:TPU:1, one launch (start us, length us, event | category | flops | bytes accessed | tf_op | source)
XLA Modules:
  0.0 733.1 jit_solution(1563439440185042986)
XLA Ops:
  6.5 0.7 all-gather.4.cloned.1.call-update
  7.3 0.5 broadcast.1194
  7.8 1.3 reduce.16
  9.2 1.1 copy.112
  10.4 0.2 convert_reduce_fusion.1
  10.6 0.7 gather_fusion.7
  11.6 0.2 convert_reduce_fusion
  11.9 0.7 copy.113
  12.6 13.0 %all-to-all-start.2 = ((s32[64,1,2]{2,1,0:T(1,128)}), s32[64,1,2]{2,1,0:T(1,128)S(1)}, u32[]{:S(2)}, u32[]{:S(2)}) async-start(s32[64,1,2]{2,1,0:T(1,128)} %copy.113), calls=%async_computation.2 | async-start | bytes 65536 | tf_op jit(solution)/shard_map/all_to_all | solution.py:151
  25.7 0.2 reduce_window_sum.18
  25.8 0.8 reshape_squeeze.6
  26.6 0.2 fusion.56
  26.8 37.0 %all-gather.4.cloned.1.call-done = bf16[1024,2048]{1,0:T(8,128)(2,1)} async-done(((bf16[1024,512]{1,0:T(8,128)(2,1)}), bf16[1024,2048]{1,0:T(8,128)(2,1)}) %all-gather.4.cloned.1.call-update) | async-done | bytes 4194320 | tf_op jit(solution)/shard_map/all_gather | solution.py:102
  63.8 11.2 %convolution_convert_fusion = bf16[1024,1536]{1,0:T(8,128)(2,1)} fusion(bf16[1024,2048]{1,0:T(8,128)(2,1)} %all-gather.4.cloned.1.call-done, bf16[2048,1536]{1,0:T(8,128)(2,1)} %param.6), kind=kOutput, calls=%fused_computation.36 | convolution fusion | flops 6444023808 | bytes 13631488 | tf_op jit(solution)/shard_map/dot_general | solution.py:101
  75.0 5.0 reshape.941
  80.0 0.4 slice.83
  80.3 1.2 copy.132
  81.6 3.4 gather_fusion
  85.0 10.9 %all-to-all-start = ((bf16[64,1,128,128]{3,2,1,0:T(8,128)(2,1)}), bf16[64,1,128,128]{3,2,1,0:T(8,128)(2,1)}, u32[]{:S(2)}, u32[]{:S(2)}) async-start(bf16[64,1,128,128]{3,2,1,0:T(8,128)(2,1)} %bitcast.166), calls=%async_computation | async-start | bytes 4194304 | tf_op jit(solution)/shard_map/all_to_all | solution.py:164
  95.9 0.2 fusion.84
  96.1 0.8 copy.153
  96.8 3.5 collective-permute-start
  100.4 0.7 copy.152
  101.1 2.1 collective-permute-start.1
  103.2 0.7 reduce.17
  104.1 0.7 slice.85
  104.8 0.5 copy.101
  105.3 38.3 %collective-permute-done = bf16[128,2,4,128]{3,0,2,1:T(8,128)(2,1)S(1)} collective-permute-done((bf16[128,2,4,128]{3,0,2,1:T(8,128)(2,1)}, bf16[128,2,4,128]{3,0,2,1:T(8,128)(2,1)S(1)}, u32[]{:S(2)}, u32[]{:S(2)}) %collective-permute-start) | collective-permute-done | bytes 262176 | tf_op jit(solution)/shard_map/ppermute | solution.py:15
  143.6 2.4 collective-permute-done.1
  146.0 1.1 pad_maximum_fusion.2
  147.2 3.8 fusion.85
  151.1 6.7 gather_fusion.8
  157.8 9.3 %all-to-all-start.3 = ((bf16[64,2,2,128,128]{4,3,2,1,0:T(8,128)(2,1)}), bf16[64,2,2,128,128]{4,3,2,1,0:T(8,128)(2,1)}, u32[]{:S(2)}, u32[]{:S(2)}) async-start(bf16[64,2,2,128,128]{4,3,2,1,0:T(8,128)(2,1)} %bitcast.161), calls=%async_computation.3 | async-start | bytes 16777216 | tf_op jit(solution)/shard_map/all_to_all | solution.py:153
  167.2 1.7 slice_select_fusion
  168.9 1.9 copy.103
  170.8 0.3 copy-done.5
  171.1 0.2 copy.105
  171.3 3.1 pad_maximum_fusion
  174.5 10.1 %gather_fusion.2 = bf16[64,3,2,128,128]{4,3,2,1,0:T(8,128)(2,1)} fusion(bf16[32,3,2,128,128]{4,3,2,0,1:T(8,128)(2,1)} %pad_maximum_fusion, s32[1024]{0:T(1024)S(1)} %pad_clamp_fusion.6), kind=kCustom, calls=%fused_computation.2 | custom fusion | bytes 25166080 | tf_op jit(solution)/shard_map/gather | solution.py:162
  184.6 217.4 %all-to-all-done.3 = bf16[64,2,2,128,128]{4,3,2,1,0:T(8,128)(2,1)} async-done(((bf16[64,2,2,128,128]{4,3,2,1,0:T(8,128)(2,1)}), bf16[64,2,2,128,128]{4,3,2,1,0:T(8,128)(2,1)}, u32[]{:S(2)}, u32[]{:S(2)}) %all-to-all-start.3) | async-done | bytes 8388640 | tf_op jit(solution)/shard_map/all_to_all | solution.py:153
  402.0 6.1 all-to-all-start.1
  408.2 0.8 gather_fusion.5
  409.5 0.2 reduce-window.8
  410.2 2.3 gather_fusion.1
  412.5 1.0 gather_fusion.6
  413.5 9.9 %gather_fusion.9 = bf16[128,2,128,128]{3,2,1,0:T(8,128)(2,1)} fusion(bf16[128,2,128,128]{3,2,1,0:T(8,128)(2,1)} %bitcast.38, s32[1024]{0:T(1024)S(1)} %pad_clamp_fusion.1), kind=kCustom, calls=%fused_computation.9 | custom fusion | bytes 16777728 | tf_op jit(solution)/shard_map/gather | solution.py:154
  423.4 6.4 gather_fusion.10
  429.8 5.2 multiply_reduce_fusion
  435.0 0.4 select_reduce_fusion.1
  435.3 248.5 %all-to-all-done.1 = bf16[64,1,3,2,128,128]{5,4,3,2,1,0:T(8,128)(2,1)} async-done(((bf16[64,1,3,2,128,128]{5,4,3,2,1,0:T(8,128)(2,1)}), bf16[64,1,3,2,128,128]{5,4,3,2,1,0:T(8,128)(2,1)}, u32[]{:S(2)}, u32[]{:S(2)}) %all-to-all-start.1) | async-done | bytes 12582944 | tf_op jit(solution)/shard_map/all_to_all | solution.py:165
  683.8 8.6 %gather_fusion.3 = bf16[32,3,2,128,128]{4,3,2,1,0:T(8,128)(2,1)} fusion(bf16[64,3,2,128,128]{4,3,2,1,0:T(8,128)(2,1)} %bitcast.27, s32[1024]{0:T(1024)S(1)} %pad_clamp_fusion.5), kind=kCustom, calls=%fused_computation.3 | custom fusion | bytes 12583040 | tf_op jit(solution)/shard_map/gather | solution.py:168
  692.4 6.8 bitcast_reduce_fusion
  699.3 1.0 gather_fusion.4
  700.2 0.1 copy.151
  700.4 6.2 fusion
  706.5 0.6 gather_fusion.11
  707.2 3.3 fusion.18
  710.4 0.2 copy-done.2
  710.6 2.7 fusion.20
  713.3 0.4 select_reduce_fusion
  713.7 0.9 copy-done.4
  714.6 2.1 fusion.1
  716.7 4.1 fusion.12
  720.9 5.4 fusion.31
  (73 shorter events, 2.1 us)
Async XLA Ops:
  6.5 401.7 %copy-start = (s32[4,512]{1,0:T(4,128)S(1)}, s32[4,512]{1,0:T(4,128)}, u32[]{:S(2)}) copy-start(s32[4,512]{1,0:T(4,128)} %param.9) | copy-start | bytes 24580
  6.5 57.3 %all-gather.4.cloned.1.call-start = ((), (), s32[]{:S(2)}) async-start(), calls=%async_computation.4 | async-start | bytes 5242880 | tf_op jit(solution)/shard_map/all_gather | solution.py:102
  10.3 1.1 copy-start.8
  12.6 72.4 %all-to-all-start.2 = ((s32[64,1,2]{2,1,0:T(1,128)}), s32[64,1,2]{2,1,0:T(1,128)S(1)}, u32[]{:S(2)}, u32[]{:S(2)}) async-start(s32[64,1,2]{2,1,0:T(1,128)} %copy.113), calls=%async_computation.2 | async-start | bytes 65536 | tf_op jit(solution)/shard_map/all_to_all | solution.py:151
  85.0 72.8 %all-to-all-start = ((bf16[64,1,128,128]{3,2,1,0:T(8,128)(2,1)}), bf16[64,1,128,128]{3,2,1,0:T(8,128)(2,1)}, u32[]{:S(2)}, u32[]{:S(2)}) async-start(bf16[64,1,128,128]{3,2,1,0:T(8,128)(2,1)} %bitcast.166), calls=%async_computation | async-start | bytes 4194304 | tf_op jit(solution)/shard_map/all_to_all | solution.py:164
  96.8 46.8 %collective-permute-start = (bf16[128,2,4,128]{3,0,2,1:T(8,128)(2,1)}, bf16[128,2,4,128]{3,0,2,1:T(8,128)(2,1)S(1)}, u32[]{:S(2)}, u32[]{:S(2)}) collective-permute-start(bf16[128,2,4,128]{3,0,2,1:T(8,128)(2,1)} %bitcast.156), channel_id=1, source_target_pairs={{0,4},{4,8},{8,12},{12,16},{16,20},{20,24},{24,28},{28,32},{32,36}... | collective-permute-start | bytes 786440 | tf_op jit(solution)/shard_map/ppermute | solution.py:15
  101.1 44.9 %collective-permute-start.1 = (bf16[128,2,4,128]{3,0,2,1:T(8,128)(2,1)}, bf16[128,2,4,128]{3,0,2,1:T(8,128)(2,1)}, u32[]{:S(2)}, u32[]{:S(2)}) collective-permute-start(bf16[128,2,4,128]{3,0,2,1:T(8,128)(2,1)} %bitcast.155), channel_id=1, source_target_pairs={{4,0},{8,4},{12,8},{16,12},{20,16},{24,20},{28,24},{32,28},{36,32}... | collective-permute-start | bytes 786440 | tf_op jit(solution)/shard_map/ppermute | solution.py:18
  147.2 3.8 copy-start.3
  157.8 244.3 %all-to-all-start.3 = ((bf16[64,2,2,128,128]{4,3,2,1,0:T(8,128)(2,1)}), bf16[64,2,2,128,128]{4,3,2,1,0:T(8,128)(2,1)}, u32[]{:S(2)}, u32[]{:S(2)}) async-start(bf16[64,2,2,128,128]{4,3,2,1,0:T(8,128)(2,1)} %bitcast.161), calls=%async_computation.3 | async-start | bytes 16777216 | tf_op jit(solution)/shard_map/all_to_all | solution.py:153
  167.1 525.3 %all-gather.6.cloned.1.call-start = ((), (), s32[]{:S(2)}) async-start(), calls=%async_computation.5 | async-start | bytes 17039360 | tf_op jit(solution)/shard_map/all_gather | solution.py:25
  168.9 2.2 copy-start.5
  402.0 7.2 copy-start.9
  402.0 281.8 %all-to-all-start.1 = ((bf16[64,1,3,2,128,128]{5,4,3,2,1,0:T(8,128)(2,1)}), bf16[64,1,3,2,128,128]{5,4,3,2,1,0:T(8,128)(2,1)}, u32[]{:S(2)}, u32[]{:S(2)}) async-start(bf16[64,1,3,2,128,128]{5,4,3,2,1,0:T(8,128)(2,1)} %bitcast.160), calls=%async_computation.1 | async-start | bytes 25165824 | tf_op jit(solution)/shard_map/all_to_all | solution.py:165
  700.4 6.2 copy-start.6
  707.1 3.4 copy-start.2
  710.6 4.0 copy-start.4
  710.6 10.2 %slice-start = ((s8[6291456]{0:T(1024)(128)(4,1)}), s8[4194304]{0:T(1024)(128)(4,1)S(1)}, s32[]{:S(2)}) async-start(s8[6291456]{0:T(1024)(128)(4,1)} %bitcast.170), calls=%async_computation.6 | async-start | bytes 8388608
  714.6 6.2 slice-start.1
  716.7 4.1 copy-start.7
  720.9 5.4 copy-start.1
Sparse Core Ops, SparseCore 0:
  9.2 54.5 all-gather.3
  170.8 216.8 all-gather.5
